TPU v7x, 1024 devices: a whole 4x4x32 slice. The times are simulated.
1024 devices in a mesh: blk: 256 (over z, x, core), node: 4 (over y).
Axes of the slice: x: 4, y: 4, z: 32, core: 2. Of those that a mesh axis runs over, the one named last changes fastest.
Arguments:
- image_embeds: bfloat16 [163840, 1152], P(('blk', 'node')), may hold values from -0.1796875 to 0.1796875
- text_embeds: bfloat16 [163840, 1152], P(('blk', 'node')), may hold values from -0.1796875 to 0.1796875
- pair_text: int32 [163840], replicated, may hold values from 0 to 163839, as said below
- similarity_scale: float32 [1], replicated, may hold values from 5 to 15
- logit_bias: float32 [1], replicated, may hold values from -6 to -2
Outputs:
- image_grads: float32 [163840, 1152], P(('blk', 'node'))
- text_grads: float32 [163840, 1152], P(('blk', 'node'))
Inputs may be any that keep to these rules, and one draw needn't show every extreme that they name: pair_text is a permutation that maps each image to a report of its own group of 640 consecutive pairs.
All inputs are finite; a program needn't handle non-finite values.
Results may differ from a plain program's by a relative error of at most 0.0043.
Values may be sent and summed in bfloat16 or wider, within the bound.
A program may use at most 32 MiB of HBM per device.

v0:
```python
import jax
import jax.numpy as jnp
from jax import lax
from jax.sharding import PartitionSpec as P

TURNS = 3


def passed_along(block, axis, distance):
    devices = range(lax.axis_size(axis))
    route = [((i - distance) % len(devices), i) for i in devices]
    return lax.ppermute(block, axis, route)


def unit_rows(raw_rows):
    values = raw_rows.astype(jnp.float32)
    inverse = lax.rsqrt(jnp.sum(values * values, axis=1, keepdims=True) + 1e-06)
    return (values * inverse, inverse)


def tangent_part(gradient, unit_rows_f, inverse):
    return (
        gradient - unit_rows_f * jnp.sum(unit_rows_f * gradient, axis=1, keepdims=True)
    ) * inverse


def pass_images(visitor):
    return passed_along(visitor, "blk", 1)


def carry_grads(partial_value):
    return passed_along(partial_value, "blk", 1)


def local(image_embeds, text_embeds, pair_text, similarity_scale, logit_bias):
    rows_here = image_embeds.shape[0]
    node_count = lax.axis_size("node")
    cycle_count = lax.axis_size("blk")
    node_index = lax.axis_index("node")
    cycle_index = lax.axis_index("blk")
    text_span = rows_here * node_count
    softness_factor = similarity_scale[0]
    shift_amount_value = logit_bias[0]
    image_unit, image_inv = unit_rows(image_embeds)
    text_unit, text_inv = unit_rows(text_embeds)
    image_half = image_unit.astype(jnp.bfloat16)
    text_half = text_unit.astype(jnp.bfloat16)
    text_block = lax.all_gather(text_half, "node", axis=0, tiled=True)
    text_start = cycle_index * text_span
    text_columns = jnp.arange(text_span, dtype=jnp.int32)
    visitor = image_half
    seen_list = []
    tile_list = []
    partial_value = jnp.zeros((rows_here, image_embeds.shape[1]), jnp.float32)
    for turn in range(TURNS):
        if turn > 0:
            visitor = pass_images(visitor)
            partial_value = carry_grads(partial_value)
        source = (cycle_index - turn + cycle_count) % cycle_count
        pair_logit_matrix = (
            softness_factor
            * lax.dot_general(
                visitor, text_block, (((1,), (1,)), ((), ())), preferred_element_type=jnp.float32
            )
            + shift_amount_value
        )
        targets = (
            lax.dynamic_slice_in_dim(
                pair_text, (source * node_count + node_index) * rows_here, rows_here, 0
            )
            - text_start
        )
        pair_label_polarity = jnp.where(
            targets[:, None] == text_columns[None, :], 1.0, -1.0
        ).astype(jnp.float32)
        weight_panel = (
            -pair_label_polarity
            * softness_factor
            * jax.nn.sigmoid(-pair_label_polarity * pair_logit_matrix)
        ).astype(jnp.bfloat16)
        term = jnp.dot(weight_panel, text_block, preferred_element_type=jnp.float32)
        partial_value = partial_value + term
        seen_list.append(visitor)
        tile_list.append(weight_panel)
    image_dir = passed_along(partial_value, "blk", -(TURNS - 1))
    seen = jnp.stack(seen_list, axis=0)
    tile_stack = jnp.stack(tile_list, axis=0)
    text_terms = jnp.einsum("sit,sid->td", tile_stack, seen, preferred_element_type=jnp.float32)
    text_dir = lax.psum_scatter(text_terms, "node", scatter_dimension=0, tiled=True)
    image_grads = tangent_part(image_dir, image_unit, image_inv)
    text_grads = tangent_part(text_dir, text_unit, text_inv)
    return (image_grads, text_grads)


def solution(mesh):
    return jax.shard_map(
        local,
        mesh=mesh,
        in_specs=(P(("blk", "node"), None), P(("blk", "node"), None), P(), P(), P()),
        out_specs=(P(("blk", "node"), None), P(("blk", "node"), None)),
        check_vma=False,
    )
```

profile of v0, /device:TPU:1, one launch (start us, length us, event | category | flops | bytes accessed | tf_op | source)
XLA Modules:
  0.0 136.2 jit_solution(9186849498721177063)
XLA Ops:
  7.2 0.0 copy-start.1
  7.2 0.0 all-gather.2.cloned.1.call-start
  7.2 1.2 fusion.42
  8.4 1.9 %fusion.31 = bf16[160,1152]{1,0:T(8,128)(2,1)} fusion(bf16[160,1152]{1,0:T(8,128)(2,1)} %param.6, f32[160]{0:T(256)S(1)} %add_rsqrt_fusion), kind=kLoop, calls=%fused_computation.38 | loop fusion | flops 552960 | bytes 737920 | tf_op jit(solution)/shard_map/convert_element_type | solution.py:47
  10.3 0.0 all-gather.2.cloned.1.call-update
  10.3 0.0 reduce-scatter.2.cloned.1.call-start
  10.3 0.0 copy-done.1
  10.4 0.2 fusion.38
  10.5 0.1 fusion.34
  10.7 4.5 %collective-permute-start.1 = (bf16[160,1152]{1,0:T(8,128)(2,1)S(1)}, bf16[160,1152]{1,0:T(8,128)(2,1)S(1)}, u32[]{:S(2)}, u32[]{:S(2)}) collective-permute-start(bf16[160,1152]{1,0:T(8,128)(2,1)S(1)} %fusion.34), channel_id=1, source_target_pairs={{1020,0},{0,4},{4,8},{8,12},{12,16},{16,20},{20,24},{24,28},{28,32... | collective-permute-start | bytes 1105928 | tf_op jit(solution)/shard_map/ppermute | solution.py:12
  16.5 0.9 dynamic-slice_subtract_fusion
  17.4 0.1 fusion.63
  17.5 10.4 %collective-permute-done.1 = bf16[160,1152]{1,0:T(8,128)(2,1)S(1)} collective-permute-done((bf16[160,1152]{1,0:T(8,128)(2,1)S(1)}, bf16[160,1152]{1,0:T(8,128)(2,1)S(1)}, u32[]{:S(2)}, u32[]{:S(2)}) %collective-permute-start.1) | collective-permute-done | bytes 368672 | tf_op jit(solution)/shard_map/ppermute | solution.py:12
  27.9 1.9 %collective-permute-start.3 = (bf16[160,1152]{1,0:T(8,128)(2,1)S(1)}, bf16[160,1152]{1,0:T(8,128)(2,1)}, u32[]{:S(2)}, u32[]{:S(2)}) collective-permute-start(bf16[160,1152]{1,0:T(8,128)(2,1)S(1)} %collective-permute-done.1), channel_id=1, source_target_pairs={{1020,0},{0,4},{4,8},{8,12},{12,16},{16,20},{20,24},{24,28},{28,32... | collective-permute-start | bytes 1105928 | tf_op jit(solution)/shard_map/ppermute | solution.py:12
  29.8 32.7 %all-gather.2.cloned.1.call-done = bf16[640,1152]{1,0:T(8,128)(2,1)} async-done(((bf16[160,1152]{1,0:T(8,128)(2,1)}), bf16[640,1152]{1,0:T(8,128)(2,1)}) %all-gather.2.cloned.1.call-update) | async-done | bytes 1474576 | tf_op jit(solution)/shard_map/all_gather | solution.py:48
  62.5 0.0 copy-start
  62.5 2.2 %fusion.21 = bf16[160,640]{1,0:T(8,128)(2,1)S(1)} fusion(bf16[160,1152]{1,0:T(8,128)(2,1)S(1)} %fusion.34, bf16[640,1152]{1,0:T(8,128)(2,1)} %all-gather.2.cloned.1.call-done, f32[]{:T(128)} %bitcast.26, f32[]{:T(128)} %bitcast.25, s32[160]{0:T(256)S(1)} %get-tuple-element.3), kind=kOutput, calls=%fused_computation.26 | convolution fusion | flops 237158400 | bytes 2048648 | tf_op jit(solution)/shard_map/dot_general | solution.py:62
  64.7 0.0 copy-done
  64.7 0.7 fusion.22
  65.3 0.0 collective-permute-done.3
  65.4 1.7 %fusion.23 = bf16[160,640]{1,0:T(8,128)(2,1)S(1)} fusion(bf16[160,1152]{1,0:T(8,128)(2,1)} %collective-permute-done.3, bf16[640,1152]{1,0:T(8,128)(2,1)S(1)} %copy-done, s32[160]{0:T(256)S(1)} %get-tuple-element.2, f32[]{:T(128)} %bitcast.27, f32[]{:T(128)} %bitcast.24), kind=kOutput, calls=%fused_computation.28 | convolution fusion | flops 237158400 | bytes 2048648 | tf_op jit(solution)/shard_map/dot_general | solution.py:62
  67.0 3.7 %convolution_bitcast_fusion = f32[640,1152]{1,0:T(8,128)} fusion(bf16[1,160,1152]{2,1,0:T(8,128)(2,1)} %bitcast.7, bf16[1,160,1152]{2,1,0:T(8,128)(2,1)S(1)} %bitcast.32, bf16[1,160,1152]{2,1,0:T(8,128)(2,1)S(1)} %fusion.63, bf16[1,160,640]{2,1,0:T(8,128)(2,1)S(1)} %bitcast.29, bf16[1,160,640]{2,1,0:T(8,128)(2,1)S(1)} %bitcast.30, ...), kind=kOutput, calls=%fused_computation | convolution fusion | flops 709509120 | bytes 4669440 | tf_op jit(solution)/shard_map/sit,sid->td/dot_general | solution.py:88
  70.7 0.0 reduce-scatter.2.cloned.1.call-update
  70.7 0.5 fusion.49
  71.2 4.4 %collective-permute-start = (f32[160,1152]{1,0:T(8,128)S(1)}, f32[160,1152]{1,0:T(8,128)S(1)}, u32[]{:S(2)}, u32[]{:S(2)}) collective-permute-start(f32[160,1152]{1,0:T(8,128)S(1)} %fusion.49), channel_id=1, source_target_pairs={{1020,0},{0,4},{4,8},{8,12},{12,16},{16,20},{20,24},{24,28},{28,32... | collective-permute-start | bytes 2211848 | tf_op jit(solution)/shard_map/ppermute | solution.py:12
  75.6 8.4 %collective-permute-done = f32[160,1152]{1,0:T(8,128)S(1)} collective-permute-done((f32[160,1152]{1,0:T(8,128)S(1)}, f32[160,1152]{1,0:T(8,128)S(1)}, u32[]{:S(2)}, u32[]{:S(2)}) %collective-permute-start) | collective-permute-done | bytes 737312 | tf_op jit(solution)/shard_map/ppermute | solution.py:12
  84.0 0.5 convolution_add_fusion
  84.5 4.4 %collective-permute-start.2 = (f32[160,1152]{1,0:T(8,128)S(1)}, f32[160,1152]{1,0:T(8,128)S(1)}, u32[]{:S(2)}, u32[]{:S(2)}) collective-permute-start(f32[160,1152]{1,0:T(8,128)S(1)} %convolution_add_fusion), channel_id=1, source_target_pairs={{1020,0},{0,4},{4,8},{8,12},{12,16},{16,20},{20,24},{24,28},{28,32... | collective-permute-start | bytes 2211848 | tf_op jit(solution)/shard_map/ppermute | solution.py:12
  88.9 0.5 fusion.50
  89.4 7.9 %collective-permute-done.2 = f32[160,1152]{1,0:T(8,128)S(1)} collective-permute-done((f32[160,1152]{1,0:T(8,128)S(1)}, f32[160,1152]{1,0:T(8,128)S(1)}, u32[]{:S(2)}, u32[]{:S(2)}) %collective-permute-start.2) | collective-permute-done | bytes 737312 | tf_op jit(solution)/shard_map/ppermute | solution.py:12
  97.3 0.1 add.112
  97.4 0.0 copy-start.2
  97.4 10.9 %collective-permute-start.4 = (f32[160,1152]{1,0:T(8,128)S(1)}, f32[160,1152]{1,0:T(8,128)S(1)}, u32[]{:S(2)}, u32[]{:S(2)}) collective-permute-start(f32[160,1152]{1,0:T(8,128)S(1)} %add.112), channel_id=1, source_target_pairs={{8,0},{12,4},{16,8},{20,12},{24,16},{28,20},{32,24},{36,28},{40,32... | collective-permute-start | bytes 2211848 | tf_op jit(solution)/shard_map/ppermute | solution.py:12
  108.3 14.9 %collective-permute-done.4 = f32[160,1152]{1,0:T(8,128)S(1)} collective-permute-done((f32[160,1152]{1,0:T(8,128)S(1)}, f32[160,1152]{1,0:T(8,128)S(1)}, u32[]{:S(2)}, u32[]{:S(2)}) %collective-permute-start.4) | collective-permute-done | bytes 737312 | tf_op jit(solution)/shard_map/ppermute | solution.py:12
  123.2 0.2 fusion.35
  123.5 1.1 fusion.37
  124.6 2.2 %reduce-scatter.2.cloned.1.call-done = f32[160,1152]{1,0:T(8,128)} async-done(((f32[640,1152]{1,0:T(8,128)}), f32[160,1152]{1,0:T(8,128)}) %reduce-scatter.2.cloned.1.call-update) | async-done | bytes 737296 | tf_op jit(solution)/shard_map/reduce_scatter | solution.py:89
  126.8 0.0 copy-done.2
  126.8 0.0 copy-start.3
  126.8 1.4 %fusion.39 = f32[160]{0:T(256)S(1)} fusion(f32[160,1152]{1,0:T(8,128)} %reduce-scatter.2.cloned.1.call-done, bf16[160,1152]{1,0:T(8,128)(2,1)S(1)} %copy-done.2, f32[160]{0:T(256)S(1)} %add_rsqrt_fusion), kind=kLoop, calls=%fused_computation.48 | loop fusion | flops 737120 | bytes 1107200 | tf_op jit(solution)/shard_map/reduce_sum | solution.py:23
  128.3 0.0 copy-done.3
  128.3 1.1 fusion.41
  (2 shorter events, 0.0 us)
Async XLA Ops:
  7.2 3.2 %copy-start.1 = (bf16[160,1152]{1,0:T(8,128)(2,1)S(1)}, bf16[160,1152]{1,0:T(8,128)(2,1)}, u32[]{:S(2)}) copy-start(bf16[160,1152]{1,0:T(8,128)(2,1)} %param.5) | copy-start | bytes 1105924
  7.2 55.3 %all-gather.2.cloned.1.call-start = ((), (), s32[]{:S(2)}) async-start(), calls=%async_computation.1 | async-start | bytes 1843200 | tf_op jit(solution)/shard_map/all_gather | solution.py:48
  10.3 116.5 %reduce-scatter.2.cloned.1.call-start = ((), (), s32[]{:S(2)}) async-start(), calls=%async_computation.2 | async-start | bytes 3686400 | tf_op jit(solution)/shard_map/reduce_scatter | solution.py:89
  10.7 17.2 %collective-permute-start.1 = (bf16[160,1152]{1,0:T(8,128)(2,1)S(1)}, bf16[160,1152]{1,0:T(8,128)(2,1)S(1)}, u32[]{:S(2)}, u32[]{:S(2)}) collective-permute-start(bf16[160,1152]{1,0:T(8,128)(2,1)S(1)} %fusion.34), channel_id=1, source_target_pairs={{1020,0},{0,4},{4,8},{8,12},{12,16},{16,20},{20,24},{24,28},{28,32... | collective-permute-start | bytes 1105928 | tf_op jit(solution)/shard_map/ppermute | solution.py:12
  27.9 37.5 %collective-permute-start.3 = (bf16[160,1152]{1,0:T(8,128)(2,1)S(1)}, bf16[160,1152]{1,0:T(8,128)(2,1)}, u32[]{:S(2)}, u32[]{:S(2)}) collective-permute-start(bf16[160,1152]{1,0:T(8,128)(2,1)S(1)} %collective-permute-done.1), channel_id=1, source_target_pairs={{1020,0},{0,4},{4,8},{8,12},{12,16},{16,20},{20,24},{24,28},{28,32... | collective-permute-start | bytes 1105928 | tf_op jit(solution)/shard_map/ppermute | solution.py:12
  62.5 2.2 %copy-start = (bf16[640,1152]{1,0:T(8,128)(2,1)S(1)}, bf16[640,1152]{1,0:T(8,128)(2,1)}, u32[]{:S(2)}) copy-start(bf16[640,1152]{1,0:T(8,128)(2,1)} %all-gather.2.cloned.1.call-done) | copy-start | bytes 4423684
  71.2 12.8 %collective-permute-start = (f32[160,1152]{1,0:T(8,128)S(1)}, f32[160,1152]{1,0:T(8,128)S(1)}, u32[]{:S(2)}, u32[]{:S(2)}) collective-permute-start(f32[160,1152]{1,0:T(8,128)S(1)} %fusion.49), channel_id=1, source_target_pairs={{1020,0},{0,4},{4,8},{8,12},{12,16},{16,20},{20,24},{24,28},{28,32... | collective-permute-start | bytes 2211848 | tf_op jit(solution)/shard_map/ppermute | solution.py:12
  84.5 12.8 %collective-permute-start.2 = (f32[160,1152]{1,0:T(8,128)S(1)}, f32[160,1152]{1,0:T(8,128)S(1)}, u32[]{:S(2)}, u32[]{:S(2)}) collective-permute-start(f32[160,1152]{1,0:T(8,128)S(1)} %convolution_add_fusion), channel_id=1, source_target_pairs={{1020,0},{0,4},{4,8},{8,12},{12,16},{16,20},{20,24},{24,28},{28,32... | collective-permute-start | bytes 2211848 | tf_op jit(solution)/shard_map/ppermute | solution.py:12
  97.4 29.5 %copy-start.2 = (bf16[160,1152]{1,0:T(8,128)(2,1)S(1)}, bf16[160,1152]{1,0:T(8,128)(2,1)}, u32[]{:S(2)}) copy-start(bf16[160,1152]{1,0:T(8,128)(2,1)} %param.6) | copy-start | bytes 1105924
  97.4 25.8 %collective-permute-start.4 = (f32[160,1152]{1,0:T(8,128)S(1)}, f32[160,1152]{1,0:T(8,128)S(1)}, u32[]{:S(2)}, u32[]{:S(2)}) collective-permute-start(f32[160,1152]{1,0:T(8,128)S(1)} %add.112), channel_id=1, source_target_pairs={{8,0},{12,4},{16,8},{20,12},{24,16},{28,20},{32,24},{36,28},{40,32... | collective-permute-start | bytes 2211848 | tf_op jit(solution)/shard_map/ppermute | solution.py:12
  126.8 1.4 %copy-start.3 = (f32[160,1152]{1,0:T(8,128)S(1)}, f32[160,1152]{1,0:T(8,128)}, u32[]{:S(2)}) copy-start(f32[160,1152]{1,0:T(8,128)} %reduce-scatter.2.cloned.1.call-done) | copy-start | bytes 2211844
Sparse Core Ops, SparseCore 0:
  11.3 51.1 all-gather.1
  70.8 55.9 reduce-scatter.1
where the time goes:
time: 137 us; the launch traced here: 136 us
  waiting for transfers between devices  76.5 us (56%)
  starting transfers between devices  26.2 us (19%)
  between operations  15.5 us (11%)
  matrix products  9.6 us (7%)
  other arithmetic  8.34 us (6%)
    ppermute x5, waiting for transfers between devices, passed_along(): return lax.ppermute(block, axis, route)  41.6 us
    all_gather x1, waiting for transfers between devices, local(): text_block = lax.all_gather(text_half, 'node', axis=0, tiled=True)  32.7 us
    ppermute x5, starting transfers between devices, passed_along(): return lax.ppermute(block, axis, route)  26.1 us
    dot_general x3, matrix products, local(): lax.dot_general(visitor, text_block, (((1,), (1,)), ((), ())), preferred_...  4.47 us
    dot_general x1, matrix products, local(): jnp.einsum('sit,sid->td', tile_stack, seen, preferred_element_type=jnp.fl...  3.68 us
  transfers between devices with their start and end apart: 7, of which 6 were waited for; matrix products, arithmetic and copies ran while one was open for 5% of the time, Pallas kernels for 0%

commit v1 on v0

v1 whole, which is shorter than its diff:
```python
import functools

import jax
import jax.numpy as jnp
from jax import lax
from jax.experimental import pallas as pl
from jax.experimental.pallas import tpu as pltpu
from jax.sharding import PartitionSpec as P

MESH = pl.DeviceIdType.MESH
CHUNKS = 2
GA, GB, GS, GX, GSF, GXF, RXP, RXO, RSP, RSO, RA_, RB_ = range(12)


def kernel(
    image_ref, text_ref, pair_ref, scale_ref, bias_ref,
    image_out, text_out,
    raw, held, ret_x, ret_s, ret_a, ret_b, got_x, got_s, got_a, got_b,
    total, inverse, pairs, scalars,
    send_sem, recv_sem, local_sem,
):
    rows, width = image_ref.shape
    part = rows // CHUNKS
    blk_count = lax.axis_size("blk")
    node_count = lax.axis_size("node")
    me = lax.axis_index("blk")
    y = lax.axis_index("node")
    core = lax.rem(me, 2)
    own = lax.rem(y, 2)
    other = 1 - own
    mate_a = y + 1 - 2 * own
    mate_b = lax.rem(y + node_count - 1 + 2 * own, node_count)
    sibling = me + 1 - 2 * core
    x_to = lax.rem(me + 4 * core - 2 + blk_count, blk_count)
    x_from = lax.rem(me - 4 * core + 2 + blk_count, blk_count)
    dev_a = (me, mate_a)
    dev_b = (me, mate_b)
    dev_s = (sibling, y)
    dev_to = (x_to, y)
    dev_from = (x_from, y)

    barrier = pltpu.get_barrier_semaphore()
    for peer in (dev_a, dev_b, dev_s, dev_to, dev_from):
        pl.semaphore_signal(barrier, inc=1, device_id=peer, device_id_type=MESH)

    load_image = pltpu.make_async_copy(image_ref, raw.at[0], local_sem.at[0])
    load_text = pltpu.make_async_copy(text_ref, raw.at[1], local_sem.at[1])
    load_pairs = pltpu.make_async_copy(
        pair_ref.at[pl.ds(pl.multiple_of(me * (rows * 4), 128), rows * 4)], pairs, local_sem.at[2]
    )
    load_scale = pltpu.make_async_copy(scale_ref, scalars.at[0], local_sem.at[3])
    load_bias = pltpu.make_async_copy(bias_ref, scalars.at[1], local_sem.at[4])
    for load in (load_image, load_text, load_pairs, load_scale, load_bias):
        load.start()

    def normalise(which):
        for k in range(5):
            at = pl.ds(k * (rows // 5), rows // 5)
            values = raw[which, at, :].astype(jnp.float32)
            inv = lax.rsqrt(jnp.sum(values * values, axis=1, keepdims=True) + 1e-06)
            inverse[which, at, :] = jnp.broadcast_to(inv, (rows // 5, 128))
            held[which, own, at, :] = (values * inv).astype(jnp.bfloat16)

    load_image.wait()
    normalise(0)
    load_text.wait()
    normalise(1)

    pl.semaphore_wait(barrier, 5)

    def remote(kind, k, src, dst, device):
        at = pl.ds(k * part, part)
        return pltpu.make_async_remote_copy(
            src_ref=src.at[at, :],
            dst_ref=dst.at[at, :],
            send_sem=send_sem.at[kind * CHUNKS + k],
            recv_sem=recv_sem.at[kind * CHUNKS + k],
            device_id=device,
            device_id_type=MESH,
        )

    def ga(k, slot):
        return remote(GA, k, held.at[0, slot], held.at[0, slot], dev_a)

    def gb(k, slot):
        return remote(GB, k, held.at[1, slot], held.at[1, slot], dev_b)

    def gs(k, slot, kind=GS):
        return remote(kind, k, held.at[1, slot], held.at[2, slot], dev_s)

    def gx(k, slot, kind=GX):
        return remote(kind, k, held.at[1 - core, slot], held.at[3, slot], dev_to)

    for k in range(CHUNKS):
        ga(k, own).start()
        gb(k, own).start()
        gx(k, own).start()
        gs(k, own).start()

    load_pairs.wait()
    load_scale.wait()
    load_bias.wait()
    scale = scalars[0, 0, 0]
    bias = scalars[1, 0, 0]

    for k in range(CHUNKS):
        gb(k, own).wait_recv()
        gs(k, other, GSF).start()

        @pl.when(core == 0)
        def _():
            gx(k, other, GXF).start()

        ga(k, own).wait_recv()

        @pl.when(core == 1)
        def _():
            gx(k, other, GXF).start()

    def both(ref):
        return ref[...].reshape(2 * rows, width)

    def weights_of(texts, images, positive=None):
        logits = scale * lax.dot_general(
            texts, images, (((1,), (1,)), ((), ())), preferred_element_type=jnp.float32
        ) + bias
        if positive is None:
            return (scale * jax.nn.sigmoid(logits)).astype(jnp.bfloat16)
        sign = jnp.where(positive, 1.0, -1.0)
        return (-sign * scale * jax.nn.sigmoid(-sign * logits)).astype(jnp.bfloat16)

    def to_texts(weights, images):
        return jnp.dot(weights, images, preferred_element_type=jnp.float32)

    def to_images(weights, texts):
        return lax.dot_general(
            weights, texts, (((0,), (0,)), ((), ())), preferred_element_type=jnp.float32
        )

    wide = pairs[...].reshape(1, 4 * rows) - me * (4 * rows)
    target = jnp.where(y < 2, wide[:, : 2 * rows], wide[:, 2 * rows :])
    even_y = jnp.where(own == 0, y, mate_b)
    odd_y = jnp.where(own == 0, mate_b, y)
    row_id = lax.broadcasted_iota(jnp.int32, (2 * rows, 1), 0)
    text_id = jnp.where(row_id < rows, row_id + even_y * rows, row_id - rows + odd_y * rows)
    positive = text_id == target

    weights = weights_of(both(held.at[1]), both(held.at[0]), positive)
    total[2] = to_texts(weights, both(held.at[0]))
    total[0] = to_images(weights, both(held.at[1]))

    for k in range(CHUNKS):
        gs(k, own).wait_recv()
        gs(k, own, GSF).wait_recv()

    @pl.when(core == 1)
    def _():
        total[1] = jnp.zeros_like(total[1])
        for k in range(CHUNKS):
            gx(k, own).wait_recv()
            gx(k, own, GXF).wait_recv()

    hub = held.at[3 * core]
    weights = weights_of(both(held.at[2]), both(hub))
    terms = to_texts(weights, both(hub)).astype(jnp.bfloat16)
    ret_s[...] = terms.reshape(2, rows, width)

    def rs(k, slot, kind):
        return remote(kind, k, ret_s.at[slot], got_s.at[slot], dev_s)

    for k in range(CHUNKS):
        rs(k, other, RSP).start()
    for k in range(CHUNKS):
        rs(k, own, RSO).start()
    total[core] += to_images(weights, both(held.at[2]))

    @pl.when(core == 0)
    def _():
        for k in range(CHUNKS):
            gx(k, own).wait_recv()
            gx(k, own, GXF).wait_recv()

    leaf = held.at[3 - 2 * core]
    weights = weights_of(both(leaf), both(hub))
    terms = to_texts(weights, both(hub))

    @pl.when(core == 0)
    def _():
        ret_x[...] = terms.astype(jnp.bfloat16).reshape(2, rows, width)

    @pl.when(core == 1)
    def _():
        total[2] += terms

    terms = to_images(weights, both(leaf))

    @pl.when(core == 0)
    def _():
        total[0] += terms

    @pl.when(core == 1)
    def _():
        ret_x[...] = (total[1] + terms).astype(jnp.bfloat16).reshape(2, rows, width)

    def rx(k, slot, kind):
        return remote(kind, k, ret_x.at[slot], got_x.at[slot], dev_from)

    def ra(k):
        return remote(RA_, k, ret_a, got_a, dev_a)

    def rb(k):
        return remote(RB_, k, ret_b, got_b, dev_b)

    for k in range(CHUNKS):
        rx(k, other, RXP).start()
    for k in range(CHUNKS):
        rx(k, own, RXO).start()

    def slot_rows(slot, k):
        return pl.ds(pl.multiple_of(slot * rows + k * part, 16), part)

    f32 = jnp.float32

    @pl.when(core == 0)
    def _():
        for k in range(CHUNKS):
            at = pl.ds(k * part, part)
            ret_a[at, :] = total[0, slot_rows(other, k), :].astype(jnp.bfloat16)
            ra(k).start()
        for k in range(CHUNKS):
            at = pl.ds(k * part, part)
            rs(k, own, RSP).wait_recv()
            rx(k, own, RXP).wait_recv()
            ret_b[at, :] = (
                total[2, slot_rows(other, k), :]
                + got_s[other, at, :].astype(f32) + got_x[other, at, :].astype(f32)
            ).astype(jnp.bfloat16)
            rb(k).start()

    @pl.when(core == 1)
    def _():
        for k in range(CHUNKS):
            at = pl.ds(k * part, part)
            rs(k, own, RSP).wait_recv()
            ret_b[at, :] = (
                total[2, slot_rows(other, k), :] + got_s[other, at, :].astype(f32)
            ).astype(jnp.bfloat16)
            rb(k).start()
        for k in range(CHUNKS):
            at = pl.ds(k * part, part)
            rx(k, own, RXP).wait_recv()
            ret_a[at, :] = (
                total[0, slot_rows(other, k), :] + got_x[other, at, :].astype(f32)
            ).astype(jnp.bfloat16)
            ra(k).start()

    def finish(which, k, extra):
        at = pl.ds(k * part, part)
        kept = total[2 * which, slot_rows(own, k), :]
        far = (got_a, got_b)[which][at, :].astype(f32)
        direction = kept + far + extra
        inv = inverse[which, at, 0:1]
        unit = raw[which, at, :].astype(f32) * inv
        along = jnp.sum(unit * direction, axis=1, keepdims=True)
        out = (image_out, text_out)[which]
        out[at, :] = (direction - unit * along) * inv

    for k in range(CHUNKS):
        at = pl.ds(k * part, part)
        rs(k, own, RSO).wait_recv()
        rx(k, own, RXO).wait_recv()
        ra(k).wait_recv()
        rb(k).wait_recv()
        from_x = got_x[own, at, :].astype(f32)
        is_odd = core == 1
        finish(0, k, jnp.where(is_odd, from_x, 0.0))
        finish(1, k, jnp.where(is_odd, 0.0, from_x) + got_s[own, at, :].astype(f32))

    for k in range(CHUNKS):
        ga(k, own).wait_send()
        gb(k, own).wait_send()
        gx(k, own).wait_send()
        gs(k, own).wait_send()
        gs(k, own, GSF).wait_send()
        gx(k, own, GXF).wait_send()
        rs(k, own, RSP).wait_send()
        rs(k, own, RSO).wait_send()
        rx(k, own, RXP).wait_send()
        rx(k, own, RXO).wait_send()
        ra(k).wait_send()
        rb(k).wait_send()


def hand_over(image_ref, text_ref, image_out, text_out, sem):
    stores = [
        pltpu.make_async_copy(image_ref, image_out, sem.at[0]),
        pltpu.make_async_copy(text_ref, text_out, sem.at[1]),
    ]
    for store in stores:
        store.start()
    for store in stores:
        store.wait()


def local(image_embeds, text_embeds, pair_text, similarity_scale, logit_bias):
    rows, width = image_embeds.shape
    any_space = pl.BlockSpec(memory_space=pl.ANY)
    bf16, f32 = jnp.bfloat16, jnp.float32
    hbm_space = pl.BlockSpec(memory_space=pltpu.HBM)
    vmem_space = pl.BlockSpec(memory_space=pltpu.VMEM)
    found = pl.pallas_call(
        kernel,
        out_shape=(pltpu.VMEM((rows, width), f32),) * 2,
        in_specs=[hbm_space] * 5,
        out_specs=(vmem_space, vmem_space),
        scratch_shapes=[
            pltpu.VMEM((2, rows, width), bf16),
            pltpu.VMEM((4, 2, rows, width), bf16),
            pltpu.VMEM((2, rows, width), bf16),
            pltpu.VMEM((2, rows, width), bf16),
            pltpu.VMEM((rows, width), bf16),
            pltpu.VMEM((rows, width), bf16),
            pltpu.VMEM((2, rows, width), bf16),
            pltpu.VMEM((2, rows, width), bf16),
            pltpu.VMEM((rows, width), bf16),
            pltpu.VMEM((rows, width), bf16),
            pltpu.VMEM((3, 2 * rows, width), f32),
            pltpu.VMEM((2, rows, 128), f32),
            pltpu.VMEM((4 * rows,), jnp.int32),
            pltpu.SMEM((2, 1, 1), f32),
            pltpu.SemaphoreType.DMA((12 * CHUNKS,)),
            pltpu.SemaphoreType.DMA((12 * CHUNKS,)),
            pltpu.SemaphoreType.DMA((5,)),
        ],
        compiler_params=pltpu.CompilerParams(collective_id=0, has_side_effects=True),
        name="pair_grads",
    )(
        image_embeds, text_embeds, pair_text,
        similarity_scale.reshape(1, 1),
        logit_bias.reshape(1, 1),
    )
    return pl.pallas_call(
        hand_over,
        out_shape=(jax.ShapeDtypeStruct((rows, width), f32),) * 2,
        in_specs=[vmem_space] * 2,
        out_specs=(any_space, any_space),
        scratch_shapes=[pltpu.SemaphoreType.DMA((2,))],
        name="hand_over",
    )(*(pltpu.with_memory_space_constraint(value, pltpu.VMEM) for value in found))


def solution(mesh):
    return jax.shard_map(
        local,
        mesh=mesh,
        in_specs=(P(("blk", "node"), None), P(("blk", "node"), None), P(), P(), P()),
        out_specs=(P(("blk", "node"), None), P(("blk", "node"), None)),
        check_vma=False,
    )
```

time: 137 us -> 55.2 us (0.40)
  the two profiles are of different devices: /device:TPU:1 before, /device:TPU:24 now
where the time goes in v1:
time: 55.2 us; the launch traced here: 55 us
  Pallas kernels  53.1 us (96%)
  between operations  1.93 us (3%)
    pallas_call x1, Pallas kernels, local(): pl.pallas_call(kernel, out_shape=(pltpu.VMEM((rows, width), f32),) * 2, i...  52 us
    pallas_call x1, Pallas kernels, local(): pl.pallas_call(hand_over, out_shape=(jax.ShapeDtypeStruct((rows, width),...  1.13 us

profile of v1, /device:TPU:24, one launch (start us, length us, event | category | flops | bytes accessed | tf_op | source)
XLA Modules:
  0.0 55.0 jit_solution(2327372593943526423)
XLA Ops:
  1.9 52.0 %pair_grads.1 = (f32[160,1152]{1,0:T(8,128)S(1)}, f32[160,1152]{1,0:T(8,128)S(1)}) custom-call(bf16[160,1152]{1,0:T(8,128)(2,1)} %image_ref.1, bf16[160,1152]{1,0:T(8,128)(2,1)} %text_ref.1, s32[163840]{0:T(1024)} %pair_ref.1, f32[1,1]{1,0:T(1,128)} %bitcast.2.scale_ref, f32[1,1]{1,0:T(1,128)} %bitcast.3.bias_ref), custom_call_target="tpu_custom_call" | custom-call | tf_op jit(solution)/shard_map/pair_grads/pallas_call | solution.py:311
  53.9 1.1 %hand_over.1 = (f32[160,1152]{1,0:T(8,128)}, f32[160,1152]{1,0:T(8,128)}) custom-call(f32[160,1152]{1,0:T(8,128)S(1)} %get-tuple-element.4.image_ref, f32[160,1152]{1,0:T(8,128)S(1)} %get-tuple-element.5.text_ref), custom_call_target="tpu_custom_call" | custom-call | tf_op jit(solution)/shard_map/hand_over/pallas_call | solution.py:342

commit v2 on v1

--- a/solution.py
+++ b/solution.py
@@ -8,8 +8,8 @@
 from jax.sharding import PartitionSpec as P
 
 MESH = pl.DeviceIdType.MESH
-CHUNKS = 2
-GA, GB, GS, GX, GSF, GXF, RXP, RXO, RSP, RSO, RA_, RB_ = range(12)
+CHUNKS = 5
+GA, GB, GS, GX, GSF, GXF, RXP, RXO, RSP, RSO, RA_, RB_, GXA = range(13)
 
 
 def kernel(
@@ -17,7 +17,7 @@
     image_out, text_out,
     raw, held, ret_x, ret_s, ret_a, ret_b, got_x, got_s, got_a, got_b,
     total, inverse, pairs, scalars,
-    send_sem, recv_sem, local_sem,
+    send_sem, recv_sem, local_sem, ready,
 ):
     rows, width = image_ref.shape
     part = rows // CHUNKS
@@ -39,9 +39,50 @@
     dev_to = (x_to, y)
     dev_from = (x_from, y)
 
+    def is_head(b):
+        return b < 2
+
+    def is_tail(b):
+        return b >= blk_count - 2
+
+    def is_first(b, n):
+        return jnp.logical_and(b == 0, n == 0)
+
+    def both_true(p, q):
+        return jnp.logical_and(p, q)
+
+    no = jnp.logical_not
+    head, tail = is_head(me), is_tail(me)
+    peers = (dev_a, dev_b, dev_s, dev_to, dev_from)
+    mirror = (0, 1, 2, 4, 3)
+    peer_late = [
+        jnp.logical_or(
+            both_true(is_first(*peer), no(tail)), both_true(is_tail(peer[0]), head)
+        )
+        for peer in peers
+    ]
+    me_late = [
+        jnp.logical_or(
+            both_true(is_first(me, y), no(is_tail(peer[0]))), both_true(tail, is_head(peer[0]))
+        )
+        for peer in peers
+    ]
+
+    swap_to = jnp.logical_or(
+        jnp.logical_and(me == 0, y != 3), jnp.logical_and(me == 2, y == 0)
+    )
+    swap_from = jnp.logical_or(
+        jnp.logical_and(me == blk_count - 2, y != 3), is_first(me, y)
+    )
+
     barrier = pltpu.get_barrier_semaphore()
-    for peer in (dev_a, dev_b, dev_s, dev_to, dev_from):
-        pl.semaphore_signal(barrier, inc=1, device_id=peer, device_id_type=MESH)
+    expected = 5
+    for r, peer in enumerate(peers):
+        @pl.when(no(me_late[r]))
+        def _():
+            pl.semaphore_signal(barrier, inc=1, device_id=peer, device_id_type=MESH)
+
+        expected = expected - jnp.where(peer_late[r], 1, 0)
 
     load_image = pltpu.make_async_copy(image_ref, raw.at[0], local_sem.at[0])
     load_text = pltpu.make_async_copy(text_ref, raw.at[1], local_sem.at[1])
@@ -66,15 +107,22 @@
     load_text.wait()
     normalise(1)
 
-    pl.semaphore_wait(barrier, 5)
-
-    def remote(kind, k, src, dst, device):
+    pl.semaphore_wait(barrier, expected)
+    for r, peer in enumerate(peers):
+        @pl.when(me_late[r])
+        def _():
+            pl.semaphore_signal(
+                ready.at[mirror[r]], inc=1, device_id=peer, device_id_type=MESH
+            )
+
+    def remote(kind, k, src, dst, device, landing=None):
+        landing = kind if landing is None else landing
         at = pl.ds(k * part, part)
         return pltpu.make_async_remote_copy(
             src_ref=src.at[at, :],
             dst_ref=dst.at[at, :],
             send_sem=send_sem.at[kind * CHUNKS + k],
-            recv_sem=recv_sem.at[kind * CHUNKS + k],
+            recv_sem=recv_sem.at[landing * CHUNKS + k],
             device_id=device,
             device_id_type=MESH,
         )
@@ -91,11 +139,44 @@
     def gx(k, slot, kind=GX):
         return remote(kind, k, held.at[1 - core, slot], held.at[3, slot], dev_to)
 
-    for k in range(CHUNKS):
-        ga(k, own).start()
-        gb(k, own).start()
-        gx(k, own).start()
-        gs(k, own).start()
+    def ga_x(k):
+        return remote(GXA, k, held.at[3, own], held.at[3, own], dev_a, GXF)
+
+    def start_own(kind):
+        for k in range(CHUNKS):
+            kind(k, own).start()
+
+    def late_sends(r, kind):
+        @pl.when(peer_late[r])
+        def _():
+            pl.semaphore_wait(ready.at[r], 1)
+            if kind is not None:
+                start_own(kind)
+
+    hold_a = both_true(tail, core == 1)
+    for r, kind in ((3, gx), (0, ga), (1, gb), (2, gs)):
+        wait_more = {3: swap_to, 0: hold_a}.get(r, False)
+
+        @pl.when(no(jnp.logical_or(peer_late[r], wait_more)))
+        def _():
+            start_own(kind)
+
+    @pl.when(hold_a)
+    def _():
+        for k in range(CHUNKS):
+            gx(k, own).wait_send()
+        start_own(ga)
+
+    for r, kind in ((0, ga), (1, gb), (2, gs)):
+        late_sends(r, kind)
+
+    @pl.when(core == 0)
+    def _():
+        late_sends(3, None)
+
+        @pl.when(both_true(peer_late[3], no(swap_to)))
+        def _():
+            start_own(gx)
 
     load_pairs.wait()
     load_scale.wait()
@@ -103,19 +184,27 @@
     scale = scalars[0, 0, 0]
     bias = scalars[1, 0, 0]
 
-    for k in range(CHUNKS):
-        gb(k, own).wait_recv()
-        gs(k, other, GSF).start()
-
-        @pl.when(core == 0)
-        def _():
-            gx(k, other, GXF).start()
-
-        ga(k, own).wait_recv()
-
-        @pl.when(core == 1)
-        def _():
-            gx(k, other, GXF).start()
+    def take_b():
+        for k in range(CHUNKS):
+            gb(k, own).wait_recv()
+
+            @pl.when(core == 0)
+            def _():
+                gx(k, other, GXF).start()
+
+            gs(k, other, GSF).start()
+
+        @pl.when(swap_to)
+        def _():
+            start_own(gx)
+
+    def take_a():
+        for k in range(CHUNKS):
+            ga(k, own).wait_recv()
+
+            @pl.when(both_true(core == 1, no(tail)))
+            def _():
+                gx(k, other, GXF).start()
 
     def both(ref):
         return ref[...].reshape(2 * rows, width)
@@ -145,88 +234,105 @@
     text_id = jnp.where(row_id < rows, row_id + even_y * rows, row_id - rows + odd_y * rows)
     positive = text_id == target
 
-    weights = weights_of(both(held.at[1]), both(held.at[0]), positive)
-    total[2] = to_texts(weights, both(held.at[0]))
-    total[0] = to_images(weights, both(held.at[1]))
-
-    for k in range(CHUNKS):
-        gs(k, own).wait_recv()
-        gs(k, own, GSF).wait_recv()
-
-    @pl.when(core == 1)
-    def _():
-        total[1] = jnp.zeros_like(total[1])
-        for k in range(CHUNKS):
-            gx(k, own).wait_recv()
-            gx(k, own, GXF).wait_recv()
-
-    hub = held.at[3 * core]
-    weights = weights_of(both(held.at[2]), both(hub))
-    terms = to_texts(weights, both(hub)).astype(jnp.bfloat16)
-    ret_s[...] = terms.reshape(2, rows, width)
+    def own_pair(first):
+        texts, images = both(held.at[1]), both(held.at[0])
+        weights = weights_of(texts, images, positive)
+        total[2] = to_texts(weights, images)
+        if first:
+            total[0] = to_images(weights, texts)
+        else:
+            total[0] += to_images(weights, texts)
+
+    def wait_sibling():
+        for k in range(CHUNKS):
+            gs(k, own).wait_recv()
+            gs(k, own, GSF).wait_recv()
 
     def rs(k, slot, kind):
         return remote(kind, k, ret_s.at[slot], got_s.at[slot], dev_s)
 
-    for k in range(CHUNKS):
-        rs(k, other, RSP).start()
-    for k in range(CHUNKS):
-        rs(k, own, RSO).start()
-    total[core] += to_images(weights, both(held.at[2]))
+    def rx(k, slot, kind):
+        return remote(kind, k, ret_x.at[slot], got_x.at[slot], dev_from)
+
+    def ra(k):
+        return remote(RA_, k, ret_a, got_a, dev_a)
+
+    def rb(k):
+        return remote(RB_, k, ret_b, got_b, dev_b)
+
+    def slot_rows(slot, k):
+        return pl.ds(pl.multiple_of(slot * rows + k * part, 16), part)
+
+    f32 = jnp.float32
+
+    bf16 = jnp.bfloat16
+    slots = ((own, GX, RXO), (other, GXF, RXP))
+
+    def return_a(extra):
+        for k in range(CHUNKS):
+            at = pl.ds(k * part, part)
+            value = total[0, slot_rows(other, k), :]
+            if extra:
+                rx(k, own, RXP).wait_recv()
+                value = value + got_x[other, at, :].astype(f32)
+            ret_a[at, :] = value.astype(bf16)
+            ra(k).start()
+
+    def ready_from():
+        @pl.when(peer_late[4])
+        def _():
+            pl.semaphore_wait(ready.at[4], 1)
+
+    order = (
+        (jnp.where(swap_from, other, own), jnp.where(swap_from, GXF, GX),
+         jnp.where(swap_from, RXP, RXO)),
+        (jnp.where(swap_from, own, other), jnp.where(swap_from, GX, GXF),
+         jnp.where(swap_from, RXO, RXP)),
+    )
+
+    def remote_texts(turn):
+        slot, kind, back = order[turn]
+        for k in range(CHUNKS):
+            gx(k, slot, kind).wait_recv()
+        images, texts = both(held.at[0]), held[3, slot]
+        weights = weights_of(texts, images)
+        ret_x[slot] = to_texts(weights, images).astype(bf16)
+        for k in range(CHUNKS):
+            rx(k, slot, back).start()
+        if turn == 0:
+            total[0] = to_images(weights, texts)
+        else:
+            total[0] += to_images(weights, texts)
 
     @pl.when(core == 0)
     def _():
-        for k in range(CHUNKS):
-            gx(k, own).wait_recv()
-            gx(k, own, GXF).wait_recv()
-
-    leaf = held.at[3 - 2 * core]
-    weights = weights_of(both(leaf), both(hub))
-    terms = to_texts(weights, both(hub))
-
-    @pl.when(core == 0)
-    def _():
-        ret_x[...] = terms.astype(jnp.bfloat16).reshape(2, rows, width)
-
-    @pl.when(core == 1)
-    def _():
-        total[2] += terms
-
-    terms = to_images(weights, both(leaf))
-
-    @pl.when(core == 0)
-    def _():
-        total[0] += terms
-
-    @pl.when(core == 1)
-    def _():
-        ret_x[...] = (total[1] + terms).astype(jnp.bfloat16).reshape(2, rows, width)
-
-    def rx(k, slot, kind):
-        return remote(kind, k, ret_x.at[slot], got_x.at[slot], dev_from)
-
-    def ra(k):
-        return remote(RA_, k, ret_a, got_a, dev_a)
-
-    def rb(k):
-        return remote(RB_, k, ret_b, got_b, dev_b)
-
-    for k in range(CHUNKS):
-        rx(k, other, RXP).start()
-    for k in range(CHUNKS):
-        rx(k, own, RXO).start()
-
-    def slot_rows(slot, k):
-        return pl.ds(pl.multiple_of(slot * rows + k * part, 16), part)
-
-    f32 = jnp.float32
-
-    @pl.when(core == 0)
-    def _():
-        for k in range(CHUNKS):
-            at = pl.ds(k * part, part)
-            ret_a[at, :] = total[0, slot_rows(other, k), :].astype(jnp.bfloat16)
-            ra(k).start()
+        @pl.when(tail)
+        def _():
+            take_a()
+            remote_texts(0)
+            take_b()
+
+        @pl.when(no(tail))
+        def _():
+            take_b()
+            take_a()
+            ready_from()
+            remote_texts(0)
+
+        own_pair(False)
+        remote_texts(1)
+        wait_sibling()
+        images, texts = both(held.at[0]), both(held.at[2])
+        weights = weights_of(texts, images)
+        ret_s[...] = to_texts(weights, images).astype(bf16).reshape(2, rows, width)
+        for k in range(CHUNKS):
+            rs(k, other, RSP).start()
+        for k in range(CHUNKS):
+            rs(k, own, RSO).start()
+        total[0] += to_images(weights, texts)
+
+        return_a(False)
+
         for k in range(CHUNKS):
             at = pl.ds(k * part, part)
             rs(k, own, RSP).wait_recv()
@@ -234,25 +340,65 @@
             ret_b[at, :] = (
                 total[2, slot_rows(other, k), :]
                 + got_s[other, at, :].astype(f32) + got_x[other, at, :].astype(f32)
-            ).astype(jnp.bfloat16)
+            ).astype(bf16)
             rb(k).start()
 
     @pl.when(core == 1)
     def _():
+        take_a()
+        take_b()
+        own_pair(True)
+        wait_sibling()
+        ready_from()
+
+        @pl.when(head)
+        def _():
+            for k in range(CHUNKS):
+                gx(k, own).wait_recv()
+                ga_x(k).start()
+
+        texts = held[1:3].reshape(4 * rows, width)
+        for slot, kind, back in slots:
+            if kind == GX:
+                @pl.when(no(head))
+                def _():
+                    for k in range(CHUNKS):
+                        gx(k, slot, kind).wait_recv()
+            else:
+                @pl.when(head)
+                def _():
+                    return_a(True)
+
+                for k in range(CHUNKS):
+                    gx(k, slot, kind).wait_recv()
+            images = held[3, slot]
+            weights = weights_of(texts, images)
+            ret_x[slot] = to_images(weights, texts).astype(bf16)
+            for k in range(CHUNKS):
+                rx(k, slot, back).start()
+            terms = to_texts(weights, images)
+            total[2] += terms[: 2 * rows]
+            if kind == GX:
+                total[1] = terms[2 * rows :]
+            else:
+                terms = total[1] + terms[2 * rows :]
+                ret_s[...] = terms.astype(bf16).reshape(2, rows, width)
+        for k in range(CHUNKS):
+            rs(k, other, RSP).start()
+        for k in range(CHUNKS):
+            rs(k, own, RSO).start()
+
         for k in range(CHUNKS):
             at = pl.ds(k * part, part)
             rs(k, own, RSP).wait_recv()
             ret_b[at, :] = (
                 total[2, slot_rows(other, k), :] + got_s[other, at, :].astype(f32)
-            ).astype(jnp.bfloat16)
+            ).astype(bf16)
             rb(k).start()
-        for k in range(CHUNKS):
-            at = pl.ds(k * part, part)
-            rx(k, own, RXP).wait_recv()
-            ret_a[at, :] = (
-                total[0, slot_rows(other, k), :] + got_x[other, at, :].astype(f32)
-            ).astype(jnp.bfloat16)
-            ra(k).start()
+
+        @pl.when(jnp.logical_not(head))
+        def _():
+            return_a(True)
 
     def finish(which, k, extra):
         at = pl.ds(k * part, part)
@@ -279,10 +425,22 @@
     for k in range(CHUNKS):
         ga(k, own).wait_send()
         gb(k, own).wait_send()
-        gx(k, own).wait_send()
         gs(k, own).wait_send()
+
+        @pl.when(no(hold_a))
+        def _():
+            gx(k, own).wait_send()
+
         gs(k, own, GSF).wait_send()
-        gx(k, own, GXF).wait_send()
+
+        @pl.when(jnp.logical_or(core == 0, no(tail)))
+        def _():
+            gx(k, own, GXF).wait_send()
+
+        @pl.when(jnp.logical_and(core == 1, head))
+        def _():
+            ga_x(k).wait_send()
+
         rs(k, own, RSP).wait_send()
         rs(k, own, RSO).wait_send()
         rx(k, own, RXP).wait_send()
@@ -328,9 +486,10 @@
             pltpu.VMEM((2, rows, 128), f32),
             pltpu.VMEM((4 * rows,), jnp.int32),
             pltpu.SMEM((2, 1, 1), f32),
-            pltpu.SemaphoreType.DMA((12 * CHUNKS,)),
-            pltpu.SemaphoreType.DMA((12 * CHUNKS,)),
+            pltpu.SemaphoreType.DMA((13 * CHUNKS,)),
+            pltpu.SemaphoreType.DMA((13 * CHUNKS,)),
             pltpu.SemaphoreType.DMA((5,)),
+            pltpu.SemaphoreType.REGULAR((5,)),
         ],
         compiler_params=pltpu.CompilerParams(collective_id=0, has_side_effects=True),
         name="pair_grads",

time: 55.2 us -> 51 us (0.924)
  Pallas kernels: 53.1 us -> 48.9 us
    pallas_call x1, Pallas kernels: 52 us -> 47.7 us  [local(): pl.pallas_call(kernel, out_shape=(pltpu.VMEM((rows, width), f32),) * 2, i...]
where the time goes in v2:
time: 51 us; the launch traced here: 50.8 us
  Pallas kernels  48.9 us (96%)
  between operations  1.93 us (4%)
    pallas_call x1, Pallas kernels, local(): pl.pallas_call(kernel, out_shape=(pltpu.VMEM((rows, width), f32),) * 2, i...  47.7 us
    pallas_call x1, Pallas kernels, local(): pl.pallas_call(hand_over, out_shape=(jax.ShapeDtypeStruct((rows, width),...  1.13 us

profile of v2, /device:TPU:24, one launch (start us, length us, event | category | flops | bytes accessed | tf_op | source)
XLA Modules:
  0.0 50.8 jit_solution(3872715812191787204)
XLA Ops:
  1.9 47.7 %pair_grads.1 = (f32[160,1152]{1,0:T(8,128)S(1)}, f32[160,1152]{1,0:T(8,128)S(1)}) custom-call(bf16[160,1152]{1,0:T(8,128)(2,1)} %image_ref.1, bf16[160,1152]{1,0:T(8,128)(2,1)} %text_ref.1, s32[163840]{0:T(1024)} %pair_ref.1, f32[1,1]{1,0:T(1,128)} %bitcast.2.scale_ref, f32[1,1]{1,0:T(1,128)} %bitcast.3.bias_ref), custom_call_target="tpu_custom_call" | custom-call | tf_op jit(solution)/shard_map/pair_grads/pallas_call | solution.py:469
  49.7 1.1 %hand_over.1 = (f32[160,1152]{1,0:T(8,128)}, f32[160,1152]{1,0:T(8,128)}) custom-call(f32[160,1152]{1,0:T(8,128)S(1)} %get-tuple-element.4.image_ref, f32[160,1152]{1,0:T(8,128)S(1)} %get-tuple-element.5.text_ref), custom_call_target="tpu_custom_call" | custom-call | tf_op jit(solution)/shard_map/hand_over/pallas_call | solution.py:501

commit v3 on v2

--- a/solution.py
+++ b/solution.py
@@ -9,7 +9,8 @@
 
 MESH = pl.DeviceIdType.MESH
 CHUNKS = 5
-GA, GB, GS, GX, GSF, GXF, RXP, RXO, RSP, RSO, RA_, RB_, GXA = range(13)
+PIECES = 1
+GA, GB, GS, GX, GSF, GXF, RXP, RXO, RSP, RSO, RA_, RB_, GXA, GW, GWA = range(15)
 
 
 def kernel(
@@ -68,12 +69,12 @@
         for peer in peers
     ]
 
-    swap_to = jnp.logical_or(
-        jnp.logical_and(me == 0, y != 3), jnp.logical_and(me == 2, y == 0)
-    )
-    swap_from = jnp.logical_or(
-        jnp.logical_and(me == blk_count - 2, y != 3), is_first(me, y)
-    )
+    swap_to = jnp.logical_and(me == 2, y == 0)
+    swap_from = is_first(me, y)
+    head_0 = both_true(head, core == 0)
+    head_1 = both_true(head, core == 1)
+    tail_0 = both_true(tail, core == 0)
+    tail_1 = both_true(tail, core == 1)
 
     barrier = pltpu.get_barrier_semaphore()
     expected = 5
@@ -153,30 +154,46 @@
             if kind is not None:
                 start_own(kind)
 
-    hold_a = both_true(tail, core == 1)
     for r, kind in ((3, gx), (0, ga), (1, gb), (2, gs)):
-        wait_more = {3: swap_to, 0: hold_a}.get(r, False)
+        wait_more = {3: swap_to, 0: tail_1}.get(r, False)
 
         @pl.when(no(jnp.logical_or(peer_late[r], wait_more)))
         def _():
             start_own(kind)
 
-    @pl.when(hold_a)
+    @pl.when(tail_1)
     def _():
         for k in range(CHUNKS):
             gx(k, own).wait_send()
         start_own(ga)
 
-    for r, kind in ((0, ga), (1, gb), (2, gs)):
-        late_sends(r, kind)
-
-    @pl.when(core == 0)
-    def _():
-        late_sends(3, None)
-
-        @pl.when(both_true(peer_late[3], no(swap_to)))
-        def _():
-            start_own(gx)
+    def gw(k):
+        return remote(GW, k, held.at[0, own], held.at[4, own], dev_from)
+
+    def straight(n):
+        return n >= 0
+
+    def gw_x(k):
+        return remote(GWA, k, held.at[0, other], held.at[4, other], dev_from)
+
+    def gw_a(k):
+        return remote(GWA, k, held.at[4, own], held.at[4, own], dev_a)
+
+    @pl.when(tail_0)
+    def _():
+        for k in range(CHUNKS):
+            ga(k, own).wait_send()
+        start_own(lambda k, slot: gw(k))
+
+    @pl.when(both_true(tail_0, straight(y)))
+    def _():
+        for k in range(CHUNKS):
+            ga(k, own).wait_recv()
+            gw_x(k).start()
+
+    @pl.when(swap_to)
+    def _():
+        pl.semaphore_wait(ready.at[3], 1)
 
     load_pairs.wait()
     load_scale.wait()
@@ -188,7 +205,7 @@
         for k in range(CHUNKS):
             gb(k, own).wait_recv()
 
-            @pl.when(core == 0)
+            @pl.when(both_true(core == 0, no(head)))
             def _():
                 gx(k, other, GXF).start()
 
@@ -196,15 +213,26 @@
 
         @pl.when(swap_to)
         def _():
+            for k in range(CHUNKS):
+                gx(k, other, GXF).wait_send()
             start_own(gx)
+            for k in range(CHUNKS):
+                gx(k, own).wait_send()
+            pl.semaphore_signal(ready.at[5], inc=1, device_id=dev_s, device_id_type=MESH)
 
     def take_a():
         for k in range(CHUNKS):
-            ga(k, own).wait_recv()
+            @pl.when(no(both_true(tail_0, straight(y))))
+            def _():
+                ga(k, own).wait_recv()
 
             @pl.when(both_true(core == 1, no(tail)))
             def _():
                 gx(k, other, GXF).start()
+
+    @pl.when(head_0)
+    def _():
+        got_x[...] = jnp.zeros_like(got_x)
 
     def both(ref):
         return ref[...].reshape(2 * rows, width)
@@ -296,31 +324,16 @@
             gx(k, slot, kind).wait_recv()
         images, texts = both(held.at[0]), held[3, slot]
         weights = weights_of(texts, images)
-        ret_x[slot] = to_texts(weights, images).astype(bf16)
-        for k in range(CHUNKS):
-            rx(k, slot, back).start()
-        if turn == 0:
-            total[0] = to_images(weights, texts)
-        else:
-            total[0] += to_images(weights, texts)
-
-    @pl.when(core == 0)
-    def _():
-        @pl.when(tail)
-        def _():
-            take_a()
-            remote_texts(0)
-            take_b()
 
         @pl.when(no(tail))
         def _():
-            take_b()
-            take_a()
-            ready_from()
-            remote_texts(0)
-
-        own_pair(False)
-        remote_texts(1)
+            ret_x[slot] = to_texts(weights, images).astype(bf16)
+            for k in range(CHUNKS):
+                rx(k, slot, back).start()
+
+        total[0] += to_images(weights, texts)
+
+    def sibling_pair():
         wait_sibling()
         images, texts = both(held.at[0]), both(held.at[2])
         weights = weights_of(texts, images)
@@ -331,74 +344,137 @@
             rs(k, own, RSO).start()
         total[0] += to_images(weights, texts)
 
-        return_a(False)
-
+    def return_b(extra):
         for k in range(CHUNKS):
             at = pl.ds(k * part, part)
             rs(k, own, RSP).wait_recv()
-            rx(k, own, RXP).wait_recv()
-            ret_b[at, :] = (
-                total[2, slot_rows(other, k), :]
-                + got_s[other, at, :].astype(f32) + got_x[other, at, :].astype(f32)
-            ).astype(bf16)
+            value = total[2, slot_rows(other, k), :] + got_s[other, at, :].astype(f32)
+            if extra:
+                rx(k, own, RXP).wait_recv()
+                value = value + got_x[other, at, :].astype(f32)
+            ret_b[at, :] = value.astype(bf16)
             rb(k).start()
 
+    @pl.when(core == 0)
+    def _():
+        late_sends(1, gb)
+        take_b()
+        late_sends(0, ga)
+
+        @pl.when(head)
+        def _():
+            pl.semaphore_wait(ready.at[3], 1)
+            start_own(gx)
+            for k in range(CHUNKS):
+                gx(k, other, GXF).start()
+
+        take_a()
+        ready_from()
+        total[0] = jnp.zeros_like(total[0])
+        first = is_first(me, y)
+
+        @pl.when(first)
+        def _():
+            sibling_pair()
+
+        remote_texts(0)
+        own_pair(False)
+        remote_texts(1)
+
+        @pl.when(no(first))
+        def _():
+            sibling_pair()
+
+        @pl.when(head)
+        def _():
+            for k in range(CHUNKS):
+                gw(k).wait_recv()
+
+                @pl.when(no(straight(mate_a)))
+                def _():
+                    gw_a(k).start()
+
+            return_a(False)
+            texts = both(held.at[1])
+            for slot in (own, other):
+                if slot is other:
+                    for k in range(CHUNKS):
+                        gw_a(k).wait_recv()
+                images = held[4, slot]
+                total[2] += to_texts(weights_of(texts, images), images)
+            return_b(False)
+
+        @pl.when(no(head))
+        def _():
+            return_a(False)
+            return_b(True)
+
     @pl.when(core == 1)
     def _():
         take_a()
+        late_sends(2, gs)
         take_b()
         own_pair(True)
         wait_sibling()
         ready_from()
 
-        @pl.when(head)
-        def _():
-            for k in range(CHUNKS):
-                gx(k, own).wait_recv()
-                ga_x(k).start()
-
         texts = held[1:3].reshape(4 * rows, width)
-        for slot, kind, back in slots:
-            if kind == GX:
-                @pl.when(no(head))
-                def _():
-                    for k in range(CHUNKS):
-                        gx(k, slot, kind).wait_recv()
-            else:
-                @pl.when(head)
-                def _():
-                    return_a(True)
-
-                for k in range(CHUNKS):
-                    gx(k, slot, kind).wait_recv()
-            images = held[3, slot]
-            weights = weights_of(texts, images)
-            ret_x[slot] = to_images(weights, texts).astype(bf16)
-            for k in range(CHUNKS):
-                rx(k, slot, back).start()
-            terms = to_texts(weights, images)
+
+        def keep_terms(terms, kind):
             total[2] += terms[: 2 * rows]
             if kind == GX:
                 total[1] = terms[2 * rows :]
             else:
-                terms = total[1] + terms[2 * rows :]
-                ret_s[...] = terms.astype(bf16).reshape(2, rows, width)
-        for k in range(CHUNKS):
-            rs(k, other, RSP).start()
-        for k in range(CHUNKS):
-            rs(k, own, RSO).start()
-
-        for k in range(CHUNKS):
-            at = pl.ds(k * part, part)
-            rs(k, own, RSP).wait_recv()
-            ret_b[at, :] = (
-                total[2, slot_rows(other, k), :] + got_s[other, at, :].astype(f32)
-            ).astype(bf16)
-            rb(k).start()
-
-        @pl.when(jnp.logical_not(head))
-        def _():
-            return_a(True)
+                total[1] += terms[2 * rows :]
+
+        def give_images(weights, slot, back):
+            ret_x[slot] = to_images(weights, texts).astype(bf16)
+            if back == RXO:
+                @pl.when(both_true(me == 3, y == 0))
+                def _():
+                    pl.semaphore_wait(ready.at[5], 1)
+
+            for k in range(CHUNKS):
+                rx(k, slot, back).start()
+
+        def give_sibling():
+            ret_s[...] = total[1].astype(bf16).reshape(2, rows, width)
+            for k in range(CHUNKS):
+                rs(k, other, RSP).start()
+            for k in range(CHUNKS):
+                rs(k, own, RSO).start()
+
+        @pl.when(head)
+        def _():
+            for k in range(CHUNKS):
+                gx(k, own).wait_recv()
+                ga_x(k).start()
+            for slot, kind, back in slots:
+                if kind != GX:
+                    for k in range(CHUNKS):
+                        gx(k, slot, kind).wait_recv()
+                images = held[3, slot]
+                weights = weights_of(texts, images)
+                keep_terms(to_texts(weights, images), kind)
+                if kind == GX:
+                    give_images(weights, slot, back)
+            return_b(False)
+            give_sibling()
+            give_images(weights, other, RXP)
+
+        @pl.when(no(head))
+        def _():
+            for slot, kind, back in slots:
+                for k in range(CHUNKS):
+                    gx(k, slot, kind).wait_recv()
+                images = held[3, slot]
+                weights = weights_of(texts, images)
+                give_images(weights, slot, back)
+                keep_terms(to_texts(weights, images), kind)
+            give_sibling()
+            return_b(False)
+
+        return_a(True)
 
     def finish(which, k, extra):
         at = pl.ds(k * part, part)
@@ -414,7 +490,11 @@
     for k in range(CHUNKS):
         at = pl.ds(k * part, part)
         rs(k, own, RSO).wait_recv()
-        rx(k, own, RXO).wait_recv()
+
+        @pl.when(no(head_0))
+        def _():
+            rx(k, own, RXO).wait_recv()
+
         ra(k).wait_recv()
         rb(k).wait_recv()
         from_x = got_x[own, at, :].astype(f32)
@@ -422,40 +502,35 @@
         finish(0, k, jnp.where(is_odd, from_x, 0.0))
         finish(1, k, jnp.where(is_odd, 0.0, from_x) + got_s[own, at, :].astype(f32))
 
+    def drained(condition, *copies):
+        @pl.when(condition)
+        def _():
+            for copy in copies:
+                copy.wait_send()
+
     for k in range(CHUNKS):
-        ga(k, own).wait_send()
-        gb(k, own).wait_send()
-        gs(k, own).wait_send()
-
-        @pl.when(no(hold_a))
-        def _():
-            gx(k, own).wait_send()
-
-        gs(k, own, GSF).wait_send()
-
-        @pl.when(jnp.logical_or(core == 0, no(tail)))
-        def _():
-            gx(k, own, GXF).wait_send()
-
-        @pl.when(jnp.logical_and(core == 1, head))
-        def _():
-            ga_x(k).wait_send()
-
-        rs(k, own, RSP).wait_send()
-        rs(k, own, RSO).wait_send()
-        rx(k, own, RXP).wait_send()
-        rx(k, own, RXO).wait_send()
-        ra(k).wait_send()
-        rb(k).wait_send()
+        for copy in (
+            gb(k, own), gs(k, own), gs(k, own, GSF), rs(k, own, RSP), rs(k, own, RSO), ra(k), rb(k)
+        ):
+            copy.wait_send()
+        drained(no(tail_0), ga(k, own), rx(k, own, RXP), rx(k, own, RXO))
+        drained(no(jnp.logical_or(swap_to, tail_1)), gx(k, own), gx(k, own, GXF))
+        drained(both_true(head_0, no(straight(mate_a))), gw_a(k))
+        drained(tail_0, gw(k))
+        drained(both_true(tail_0, straight(y)), gw_x(k))
+        drained(head_1, ga_x(k))
 
 
 def hand_over(image_ref, text_ref, image_out, text_out, sem):
-    stores = [
-        pltpu.make_async_copy(image_ref, image_out, sem.at[0]),
-        pltpu.make_async_copy(text_ref, text_out, sem.at[1]),
-    ]
-    for store in stores:
-        store.start()
+    part = image_ref.shape[0] // PIECES
+    stores = []
+    for k in range(PIECES):
+        at = pl.ds(k * part, part)
+        for which, (src, dst) in enumerate(((image_ref, image_out), (text_ref, text_out))):
+            stores.append(
+                pltpu.make_async_copy(src.at[at, :], dst.at[at, :], sem.at[2 * k + which])
+            )
+            stores[-1].start()
     for store in stores:
         store.wait()
 
@@ -473,7 +548,7 @@
         out_specs=(vmem_space, vmem_space),
         scratch_shapes=[
             pltpu.VMEM((2, rows, width), bf16),
-            pltpu.VMEM((4, 2, rows, width), bf16),
+            pltpu.VMEM((5, 2, rows, width), bf16),
             pltpu.VMEM((2, rows, width), bf16),
             pltpu.VMEM((2, rows, width), bf16),
             pltpu.VMEM((rows, width), bf16),
@@ -486,10 +561,10 @@
             pltpu.VMEM((2, rows, 128), f32),
             pltpu.VMEM((4 * rows,), jnp.int32),
             pltpu.SMEM((2, 1, 1), f32),
-            pltpu.SemaphoreType.DMA((13 * CHUNKS,)),
-            pltpu.SemaphoreType.DMA((13 * CHUNKS,)),
+            pltpu.SemaphoreType.DMA((15 * CHUNKS,)),
+            pltpu.SemaphoreType.DMA((15 * CHUNKS,)),
             pltpu.SemaphoreType.DMA((5,)),
-            pltpu.SemaphoreType.REGULAR((5,)),
+            pltpu.SemaphoreType.REGULAR((6,)),
         ],
         compiler_params=pltpu.CompilerParams(collective_id=0, has_side_effects=True),
         name="pair_grads",
@@ -503,7 +578,7 @@
         out_shape=(jax.ShapeDtypeStruct((rows, width), f32),) * 2,
         in_specs=[vmem_space] * 2,
         out_specs=(any_space, any_space),
-        scratch_shapes=[pltpu.SemaphoreType.DMA((2,))],
+        scratch_shapes=[pltpu.SemaphoreType.DMA((2 * PIECES,))],
         name="hand_over",
     )(*(pltpu.with_memory_space_constraint(value, pltpu.VMEM) for value in found))
 

time: 51 us -> 49.7 us (0.975)
  Pallas kernels: 48.9 us -> 47.4 us
    pallas_call x1, Pallas kernels: 47.7 us -> 46.3 us  [local(): pl.pallas_call(kernel, out_shape=(pltpu.VMEM((rows, width), f32),) * 2, i...]
where the time goes in v3:
time: 49.7 us; the launch traced here: 49.5 us
  Pallas kernels  47.4 us (95%)
  between operations  2.11 us (4%)
    pallas_call x1, Pallas kernels, local(): pl.pallas_call(kernel, out_shape=(pltpu.VMEM((rows, width), f32),) * 2, i...  46.3 us
    pallas_call x1, Pallas kernels, local(): pl.pallas_call(hand_over, out_shape=(jax.ShapeDtypeStruct((rows, width),...  1.13 us

profile of v3, /device:TPU:24, one launch (start us, length us, event | category | flops | bytes accessed | tf_op | source)
XLA Modules:
  0.0 49.5 jit_solution(8070042897029076729)
XLA Ops:
  1.9 46.3 %pair_grads.1 = (f32[160,1152]{1,0:T(8,128)S(1)}, f32[160,1152]{1,0:T(8,128)S(1)}) custom-call(bf16[160,1152]{1,0:T(8,128)(2,1)} %image_ref.1, bf16[160,1152]{1,0:T(8,128)(2,1)} %text_ref.1, s32[163840]{0:T(1024)} %pair_ref.1, f32[1,1]{1,0:T(1,128)} %bitcast.2.scale_ref, f32[1,1]{1,0:T(1,128)} %bitcast.3.bias_ref), custom_call_target="tpu_custom_call" | custom-call | tf_op jit(solution)/shard_map/pair_grads/pallas_call | solution.py:544
  48.2 1.1 %hand_over.1 = (f32[160,1152]{1,0:T(8,128)}, f32[160,1152]{1,0:T(8,128)}) custom-call(f32[160,1152]{1,0:T(8,128)S(1)} %get-tuple-element.4.image_ref, f32[160,1152]{1,0:T(8,128)S(1)} %get-tuple-element.5.text_ref), custom_call_target="tpu_custom_call" | custom-call | tf_op jit(solution)/shard_map/hand_over/pallas_call | solution.py:576
